TPU v7x, 32 devices: a whole 2x2x4 slice. The times are simulated.
32 devices in a mesh: groups: 2 (over y), feat: 4 (over z), dp: 2 (over x), section: 2 (over core).
Axes of the slice: x: 2, y: 2, z: 4, core: 2. Of those that a mesh axis runs over, the one named last changes fastest.
Arguments:
- residuals: bfloat16 [2, 3072, 8192], P('section', ('groups', 'dp'), 'feat'), parts along dimension 1, may hold values from -6 to 6
- final_resid: bfloat16 [3072, 8192], P(('groups', 'dp', 'section'), 'feat'), parts along dimension 0, may hold values from -6 to 6
- final_order: int32 [3072], P(('groups', 'dp')), parts along dimension 0, may hold values from 0 to 767, as said below
- translator: bfloat16 [2, 8192, 8192], P('section', 'dp', 'feat'), may hold values from -0.0625 to 0.0625
- bias: float32 [2, 8192], P('section', 'feat'), may hold values from -5 to 5
Outputs:
- grad_weight: bfloat16 [4, 8192, 8192], P(('groups', 'section'), 'dp', 'feat'), parts along dimension 0
- grad_bias: float32 [4, 8192], P(('groups', 'section'), 'feat'), parts along dimension 0
There are 2 independent parts, one for each index of `groups`. A program takes and returns all parts, laid end to end along the dimension named above; an argument that names none is the same for every part. Nothing has to cross between parts.
Inputs may be any that keep to these rules, and one draw needn't show every extreme that they name: Within each aligned block of 768 tokens final_order is a permutation of 0 to 767.
All inputs are finite; a program needn't handle non-finite values.
Results may differ from a plain program's by a relative error of at most 0.0058.
Values may be sent and summed in bfloat16 or wider, within the bound.
A program may use at most 192 MiB of HBM per device.

v0:
```python
import math
import jax
import jax.numpy as jnp
from jax import lax
from jax.sharding import PartitionSpec as P


def on_device(residuals, final_resid, final_order, translator, bias):
    layer_rows = residuals[0]
    local_weight = translator[0]
    gathered_final = lax.all_gather(final_resid, "section", axis=0, tiled=True)
    targets = gathered_final[final_order].astype(jnp.float32)
    full_weight = lax.all_gather(local_weight, "dp", axis=0, tiled=True)
    gathered = lax.all_gather(layer_rows, "feat", axis=1, tiled=True)
    product = jnp.dot(gathered, full_weight, preferred_element_type=jnp.float32)
    predicted = layer_rows.astype(jnp.float32) + product + bias[0]
    token_total = layer_rows.shape[0] * lax.axis_size("dp")
    factor = 1.0 / math.sqrt(token_total)
    scaled_error = (predicted - targets) * factor
    grad_b = lax.psum(jnp.sum(scaled_error, axis=0), "dp")
    rounded = scaled_error.astype(jnp.bfloat16)
    partial_sum = lax.dot_general(
        gathered, rounded, (((0,), (0,)), ((), ())), preferred_element_type=jnp.float32
    )
    partial_sum = lax.optimization_barrier(partial_sum.astype(jnp.bfloat16))
    grad_w = lax.psum_scatter(
        partial_sum.astype(jnp.float32).astype(jnp.bfloat16), "dp", scatter_dimension=0, tiled=True
    )
    return (grad_w[None], grad_b[None])


def solution(mesh):
    placed = (
        P("section", ("groups", "dp"), "feat"),
        P(("groups", "dp", "section"), "feat"),
        P(("groups", "dp")),
        P("section", "dp", "feat"),
        P("section", "feat"),
    )
    return jax.shard_map(
        on_device,
        mesh=mesh,
        in_specs=placed,
        out_specs=(P(("groups", "section"), "dp", "feat"), P(("groups", "section"), "feat")),
        check_vma=False,
    )
```

profile of v0, /device:TPU:0, one launch (start us, length us, event | category | flops | bytes accessed | tf_op | source)
XLA Modules:
  0.0 1101.7 jit_solution(1509310580802462595)
XLA Ops:
  7.2 0.0 all-gather.6.cloned.1.call-start
  7.2 0.7 all-gather.6.cloned.1.call-update
  7.9 0.0 all-gather.8.cloned.1.call-start
  7.9 0.7 all-gather.8.cloned.1.call-update
  8.6 0.0 copy-start.1
  8.7 0.0 all-gather.10.cloned.1.call-start
  8.7 0.7 all-gather.10.cloned.1.call-update
  9.4 0.0 reduce-scatter.2.cloned.1.call-start
  9.4 0.0 copy-done.1
  9.5 0.0 copy-start
  9.5 0.0 copy-start.2
  9.5 14.9 %all-gather.6.cloned.1.call-done = bf16[768,2048]{1,0:T(8,128)(2,1)} async-done(((bf16[384,2048]{1,0:T(8,128)(2,1)}), bf16[768,2048]{1,0:T(8,128)(2,1)}) %all-gather.6.cloned.1.call-update) | async-done | bytes 3145744 | tf_op jit(solution)/shard_map/all_gather | solution.py:11
  24.4 9.4 gather_fusion
  33.8 211.6 %all-gather.8.cloned.1.call-done = bf16[1,768,8192]{2,1,0:T(8,128)(2,1)} async-done(((bf16[1,768,2048]{2,1,0:T(8,128)(2,1)}), bf16[1,768,8192]{2,1,0:T(8,128)(2,1)}) %all-gather.8.cloned.1.call-update) | async-done | bytes 12582928 | tf_op jit(solution)/shard_map/all_gather | solution.py:14
  245.4 388.3 %all-gather.10.cloned.1.call-done = bf16[1,8192,2048]{2,1,0:T(8,128)(2,1)} async-done(((bf16[1,4096,2048]{2,1,0:T(8,128)(2,1)}), bf16[1,8192,2048]{2,1,0:T(8,128)(2,1)}) %all-gather.10.cloned.1.call-update) | async-done | bytes 33554448 | tf_op jit(solution)/shard_map/all_gather | solution.py:13
  633.7 0.0 copy-done
  633.7 0.0 copy-done.2
  633.7 34.7 %fusion.12 = (f32[2048]{0:T(1024)S(1)}, bf16[768,2048]{1,0:T(8,128)(2,1)S(1)}) fusion(bf16[768,2048]{1,0:T(8,128)(2,1)} %gather_fusion, f32[2048]{0:T(1024)S(1)} %bitcast.27, bf16[1,8192,2048]{2,1,0:T(8,128)(2,1)} %all-gather.10.cloned.1.call-done, bf16[1,768,8192]{2,1,0:T(8,128)(2,1)} %all-gather.8.cloned.1.call-done, bf16[1,768,2048]{2,1,0:T(8,128)(2,1)S(1)} %copy-done), kind=kOutput, calls=%fused_computation.13 | convolution fusion | flops 25782384640 | bytes 55590912 | tf_op jit(solution)/shard_map/dot_general | solution.py:15
  668.4 35.2 %convert_bitcast_fusion = bf16[8192,2048]{0,1:T(8,128)(2,1)} fusion(bf16[1,768,8192]{2,1,0:T(8,128)(2,1)} %all-gather.8.cloned.1.call-done, bf16[768,2048]{1,0:T(8,128)(2,1)S(1)} %get-tuple-element.5), kind=kOutput, calls=%fused_computation.3 | convolution fusion | flops 25786580992 | bytes 49283072 | tf_op jit(solution)/shard_map/dot_general | solution.py:22
  703.6 0.0 reduce-scatter.2.cloned.1.call-update
  703.7 5.6 psum.7
  709.3 363.5 %reduce-scatter.2.cloned.1.call-done = bf16[4096,2048]{0,1:T(8,128)(2,1)} async-done(((bf16[8192,2048]{0,1:T(8,128)(2,1)}), bf16[4096,2048]{0,1:T(8,128)(2,1)}) %reduce-scatter.2.cloned.1.call-update) | async-done | bytes 16777232 | tf_op jit(solution)/shard_map/reduce_scatter | solution.py:26
  1072.7 22.4 %copy.7 = bf16[1,4096,2048]{2,1,0:T(8,128)(2,1)} copy(bf16[1,4096,2048]{1,2,0:T(8,128)(2,1)} %bitcast.25) | data formatting | bytes 33554432
  (2 shorter events, 0.0 us)
Async XLA Ops:
  7.2 17.2 %all-gather.6.cloned.1.call-start = ((), (), s32[]{:S(2)}) async-start(), calls=%async_computation.1 | async-start | bytes 4718592 | tf_op jit(solution)/shard_map/all_gather | solution.py:11
  7.9 237.5 %all-gather.8.cloned.1.call-start = ((), (), s32[]{:S(2)}) async-start(), calls=%async_computation.3 | async-start | bytes 15728640 | tf_op jit(solution)/shard_map/all_gather | solution.py:14
  8.6 0.8 copy-start.1
  8.7 625.1 %all-gather.10.cloned.1.call-start = ((), (), s32[]{:S(2)}) async-start(), calls=%async_computation.4 | async-start | bytes 50331648 | tf_op jit(solution)/shard_map/all_gather | solution.py:13
  9.4 1063.3 %reduce-scatter.2.cloned.1.call-start = ((), (), s32[]{:S(2)}) async-start(), calls=%async_computation.2 | async-start | bytes 50331648 | tf_op jit(solution)/shard_map/reduce_scatter | solution.py:26
  9.5 624.2 %copy-start = (bf16[1,768,2048]{2,1,0:T(8,128)(2,1)S(1)}, bf16[1,768,2048]{2,1,0:T(8,128)(2,1)}, u32[]{:S(2)}) copy-start(bf16[1,768,2048]{2,1,0:T(8,128)(2,1)} %param.5) | copy-start | bytes 9437188
  9.5 624.2 %copy-start.2 = (f32[1,2048]{1,0:T(1,128)S(1)}, f32[1,2048]{1,0:T(1,128)}, u32[]{:S(2)}) copy-start(f32[1,2048]{1,0:T(1,128)} %param.9) | copy-start | bytes 24580
Sparse Core Ops, SparseCore 0:
  9.5 14.8 all-gather.5
  26.0 219.3 all-gather.7
  246.9 386.7 all-gather.9
  703.8 368.8 reduce-scatter.1
where the time goes:
time: 1100 us
  waiting for transfers between devices  980 us (89%)
  matrix products  69.9 us (6%)
  local copies, waits for them, and re-layouts  31.8 us (3%)
  between operations  13.8 us (1%)
    all_gather x1, waiting for transfers between devices, on_device(): full_weight = lax.all_gather(local_weight, 'dp', axis=0, tiled=True)  388 us
    reduce_scatter x1, waiting for transfers between devices, on_device(): lax.psum_scatter(partial_sum.astype(jnp.float32).astype(jnp.bfloat16), 'd...  363 us
    all_gather x1, waiting for transfers between devices, on_device(): gathered = lax.all_gather(layer_rows, 'feat', axis=1, tiled=True)  212 us
    dot_general x1, matrix products, on_device(): lax.dot_general(gathered, rounded, (((0,), (0,)), ((), ())), preferred_el...  35.2 us
    dot_general x1, matrix products, on_device(): product = jnp.dot(gathered, full_weight, preferred_element_type=jnp.float32)  34.7 us
    unnamed x7, local copies, waits for them, and re-layouts  22.4 us
  transfers between devices with their start and end apart: 4, of which 4 were waited for; matrix products, arithmetic and copies ran while one was open for 1% of the time, Pallas kernels for 0%

commit v1 on v0

--- a/solution.py
+++ b/solution.py
@@ -3,6 +3,20 @@
 import jax.numpy as jnp
 from jax import lax
 from jax.sharding import PartitionSpec as P
+from jax.lax import axis_index, axis_size, ppermute
+
+
+def draw_signs(page):
+    row_axis = "feat"
+    width = axis_size(row_axis)
+    trail = tuple(((to_i, (to_i + 1) % width) for to_i in range(width)))
+    raw_out = [None] * width
+    raw_out[width - 1] = page
+    for m in range(width - 2, -1, -1):
+        raw_out[m] = ppermute(raw_out[m + 1], row_axis, trail)
+    back = jnp.concatenate(raw_out, 1)
+    last = (axis_index(row_axis) + 1) * page.shape[1]
+    return jnp.roll(back, last, 1)
 
 
 def on_device(residuals, final_resid, final_order, translator, bias):
@@ -11,7 +25,7 @@
     gathered_final = lax.all_gather(final_resid, "section", axis=0, tiled=True)
     targets = gathered_final[final_order].astype(jnp.float32)
     full_weight = lax.all_gather(local_weight, "dp", axis=0, tiled=True)
-    gathered = lax.all_gather(layer_rows, "feat", axis=1, tiled=True)
+    gathered = draw_signs(layer_rows)
     product = jnp.dot(gathered, full_weight, preferred_element_type=jnp.float32)
     predicted = layer_rows.astype(jnp.float32) + product + bias[0]
     token_total = layer_rows.shape[0] * lax.axis_size("dp")

time: 1100 us -> 861 us (0.78)
  waiting for transfers between devices: 980 us -> 734 us
    all_gather x1, waiting for transfers between devices: 388 us -> 167 us  [on_device(): full_weight = lax.all_gather(local_weight, 'dp', axis=0, tiled=True)]
    all_gather x1 -> x0, waiting for transfers between devices: 212 us -> none  [on_device(): gathered = lax.all_gather(layer_rows, 'feat', axis=1, tiled=True)]
    ppermute x0 -> x3, waiting for transfers between devices: none -> 202 us  [draw_signs(): raw_out[m] = ppermute(raw_out[m + 1], row_axis, trail)]
    all_gather x1, waiting for transfers between devices: 14.9 us -> 0.02 us  [on_device(): gathered_final = lax.all_gather(final_resid, 'section', axis=0, tiled=True)]
    unnamed x7 -> x17, local copies, waits for them, and re-layouts: 22.4 us -> 23.6 us
  transfers between devices with their start and end apart: 4 -> 6, of which waited for: 4 -> 5; matrix products, arithmetic and copies ran while one was open for 1% -> 4% of each run, Pallas kernels for 0% -> 0%
where the time goes in v1:
time: 861 us
  waiting for transfers between devices  734 us (85%)
  matrix products  69.7 us (8%)
  local copies, waits for them, and re-layouts  34.9 us (4%)
  between operations  13.8 us (2%)
    reduce_scatter x1, waiting for transfers between devices, on_device(): lax.psum_scatter(partial_sum.astype(jnp.float32).astype(jnp.bfloat16), 'd...  363 us
    ppermute x3, waiting for transfers between devices, draw_signs(): raw_out[m] = ppermute(raw_out[m + 1], row_axis, trail)  202 us
    all_gather x1, waiting for transfers between devices, on_device(): full_weight = lax.all_gather(local_weight, 'dp', axis=0, tiled=True)  167 us
    dot_general x1, matrix products, on_device(): lax.dot_general(gathered, rounded, (((0,), (0,)), ((), ())), preferred_el...  35 us
    dot_general x1, matrix products, on_device(): product = jnp.dot(gathered, full_weight, preferred_element_type=jnp.float32)  34.7 us
    unnamed x17, local copies, waits for them, and re-layouts  23.6 us
  transfers between devices with their start and end apart: 6, of which 5 were waited for; matrix products, arithmetic and copies ran while one was open for 4% of the time, Pallas kernels for 0%

profile of v1, /device:TPU:0, one launch (start us, length us, event | category | flops | bytes accessed | tf_op | source)
XLA Modules:
  0.0 861.1 jit_solution(16034260441950724348)
XLA Ops:
  7.2 0.0 copy-start
  7.2 0.0 copy-start.3
  7.2 0.0 all-gather.4.cloned.1.call-start
  7.2 0.7 all-gather.4.cloned.1.call-update
  7.9 0.0 all-gather.6.cloned.1.call-start
  8.0 0.7 all-gather.6.cloned.1.call-update
  8.7 0.0 reduce-scatter.2.cloned.1.call-start
  8.7 0.3 copy-done
  9.1 3.0 collective-permute-start
  12.1 70.1 %collective-permute-done = bf16[768,2048]{1,0:T(8,128)(2,1)S(1)} collective-permute-done((bf16[768,2048]{1,0:T(8,128)(2,1)S(1)}, bf16[768,2048]{1,0:T(8,128)(2,1)S(1)}, u32[]{:S(2)}, u32[]{:S(2)}) %collective-permute-start) | collective-permute-done | bytes 3145760 | tf_op jit(solution)/shard_map/ppermute | solution.py:16
  82.2 0.0 copy-start.1
  82.2 1.7 copy-done.1
  83.9 0.0 collective-permute-start.1
  83.9 71.2 %collective-permute-done.1 = bf16[768,2048]{1,0:T(8,128)(2,1)} collective-permute-done((bf16[768,2048]{1,0:T(8,128)(2,1)S(1)}, bf16[768,2048]{1,0:T(8,128)(2,1)}, u32[]{:S(2)}, u32[]{:S(2)}) %collective-permute-start.1) | collective-permute-done | bytes 3145760 | tf_op jit(solution)/shard_map/ppermute | solution.py:16
  155.1 0.0 collective-permute-start.2
  155.1 0.0 copy-done.3
  155.1 0.0 all-gather.4.cloned.1.call-done
  155.1 9.4 %gather_fusion = bf16[768,2048]{1,0:T(8,128)(2,1)} fusion(bf16[768,2048]{1,0:T(8,128)(2,1)} %all-gather.4.cloned.1.call-done, s32[1024]{0:T(1024)S(1)} %pad_clamp_fusion), kind=kCustom, calls=%fused_computation | custom fusion | bytes 6294528 | tf_op jit(solution)/shard_map/gather | solution.py:26
  164.5 0.0 copy-start.2
  164.5 61.0 %collective-permute-done.2 = bf16[768,2048]{1,0:T(8,128)(2,1)} collective-permute-done((bf16[768,2048]{1,0:T(8,128)(2,1)}, bf16[768,2048]{1,0:T(8,128)(2,1)}, u32[]{:S(2)}, u32[]{:S(2)}) %collective-permute-start.2) | collective-permute-done | bytes 3145760 | tf_op jit(solution)/shard_map/ppermute | solution.py:16
  225.5 3.9 constant_dynamic-update-slice_fusion.7
  229.4 3.9 constant_dynamic-update-slice_fusion.6
  233.3 0.0 copy-done.2
  233.3 2.0 constant_dynamic-update-slice_fusion.5
  235.3 2.0 constant_dynamic-update-slice_fusion.4
  237.3 0.0 copy-start.4
  237.3 3.9 constant_dynamic-update-slice_fusion.3
  241.2 3.9 constant_dynamic-update-slice_fusion.2
  245.1 2.0 constant_dynamic-update-slice_fusion.1
  247.1 2.0 constant_dynamic-update-slice_fusion
  249.1 166.7 %all-gather.6.cloned.1.call-done = bf16[1,8192,2048]{2,1,0:T(8,128)(2,1)} async-done(((bf16[1,4096,2048]{2,1,0:T(8,128)(2,1)}), bf16[1,8192,2048]{2,1,0:T(8,128)(2,1)}) %all-gather.6.cloned.1.call-update) | async-done | bytes 33554448 | tf_op jit(solution)/shard_map/all_gather | solution.py:27
  415.7 0.0 copy-done.4
  415.7 34.7 %fusion.11 = (f32[2048]{0:T(1024)S(1)}, bf16[768,2048]{1,0:T(8,128)(2,1)S(1)}) fusion(bf16[768,2048]{1,0:T(8,128)(2,1)} %gather_fusion, f32[2048]{0:T(1024)S(1)} %bitcast.18, bf16[1,8192,2048]{2,1,0:T(8,128)(2,1)} %all-gather.6.cloned.1.call-done, bf16[768,16384]{1,0:T(8,128)(2,1)} %constant_dynamic-update-slice_fusion, s32[]{:T(128)S(6)} %select_n.17, ...), kind=kOutput, calls=%fused_computation.20 | convolution fusion | flops 25782384640 | bytes 55590916 | tf_op jit(solution)/shard_map/dot_general | solution.py:29
  450.4 35.0 %convolution_convert_fusion = bf16[8192,2048]{1,0:T(8,128)(2,1)} fusion(bf16[768,16384]{1,0:T(8,128)(2,1)} %constant_dynamic-update-slice_fusion, s32[]{:T(128)S(6)} %select_n.17, bf16[768,2048]{1,0:T(8,128)(2,1)S(1)} %get-tuple-element.3), kind=kOutput, calls=%fused_computation.3 | convolution fusion | flops 25786580992 | bytes 49283076 | tf_op jit(solution)/shard_map/dot_general | solution.py:36
  485.5 0.0 reduce-scatter.2.cloned.1.call-update
  485.5 5.6 psum.7
  491.1 363.5 %reduce-scatter.2.cloned.1.call-done = bf16[4096,2048]{1,0:T(8,128)(2,1)} async-done(((bf16[8192,2048]{1,0:T(8,128)(2,1)}), bf16[4096,2048]{1,0:T(8,128)(2,1)}) %reduce-scatter.2.cloned.1.call-update) | async-done | bytes 16777232 | tf_op jit(solution)/shard_map/reduce_scatter | solution.py:40
  (2 shorter events, 0.0 us)
Async XLA Ops:
  7.2 1.9 copy-start
  7.2 147.9 %copy-start.3 = (s32[768]{0:T(1024)S(1)}, s32[768]{0:T(1024)}, u32[]{:S(2)}) copy-start(s32[768]{0:T(1024)} %param.7) | copy-start | bytes 9220
  7.2 147.9 %all-gather.4.cloned.1.call-start = ((), (), s32[]{:S(2)}) async-start(), calls=%async_computation.1 | async-start | bytes 4718592 | tf_op jit(solution)/shard_map/all_gather | solution.py:25
  7.9 407.8 %all-gather.6.cloned.1.call-start = ((), (), s32[]{:S(2)}) async-start(), calls=%async_computation.3 | async-start | bytes 50331648 | tf_op jit(solution)/shard_map/all_gather | solution.py:27
  8.7 845.9 %reduce-scatter.2.cloned.1.call-start = ((), (), s32[]{:S(2)}) async-start(), calls=%async_computation.2 | async-start | bytes 50331648 | tf_op jit(solution)/shard_map/reduce_scatter | solution.py:40
  9.1 73.1 %collective-permute-start = (bf16[768,2048]{1,0:T(8,128)(2,1)S(1)}, bf16[768,2048]{1,0:T(8,128)(2,1)S(1)}, u32[]{:S(2)}, u32[]{:S(2)}) collective-permute-start(bf16[768,2048]{1,0:T(8,128)(2,1)S(1)} %bitcast.15), channel_id=1, source_target_pairs={{0,4},{4,8},{8,12},{12,0},{1,5},{5,9},{9,13},{13,1},{2,6},{6,10},{... | collective-permute-start | bytes 9437192 | tf_op jit(solution)/shard_map/ppermute | solution.py:16
  82.2 1.7 copy-start.1
  83.9 71.2 %collective-permute-start.1 = (bf16[768,2048]{1,0:T(8,128)(2,1)S(1)}, bf16[768,2048]{1,0:T(8,128)(2,1)}, u32[]{:S(2)}, u32[]{:S(2)}) collective-permute-start(bf16[768,2048]{1,0:T(8,128)(2,1)S(1)} %collective-permute-done), channel_id=1, source_target_pairs={{0,4},{4,8},{8,12},{12,0},{1,5},{5,9},{9,13},{13,1},{2,6},{6,10},{... | collective-permute-start | bytes 9437192 | tf_op jit(solution)/shard_map/ppermute | solution.py:16
  155.1 70.5 %collective-permute-start.2 = (bf16[768,2048]{1,0:T(8,128)(2,1)}, bf16[768,2048]{1,0:T(8,128)(2,1)}, u32[]{:S(2)}, u32[]{:S(2)}) collective-permute-start(bf16[768,2048]{1,0:T(8,128)(2,1)} %collective-permute-done.1), channel_id=1, source_target_pairs={{0,4},{4,8},{8,12},{12,0},{1,5},{5,9},{9,13},{13,1},{2,6},{6,10},{... | collective-permute-start | bytes 9437192 | tf_op jit(solution)/shard_map/ppermute | solution.py:16
  164.5 68.8 %copy-start.2 = (bf16[768,2048]{1,0:T(8,128)(2,1)S(1)}, bf16[768,2048]{1,0:T(8,128)(2,1)}, u32[]{:S(2)}) copy-start(bf16[768,2048]{1,0:T(8,128)(2,1)} %copy-done.1) | copy-start | bytes 9437188
  237.3 178.4 %copy-start.4 = (f32[1,2048]{1,0:T(1,128)S(1)}, f32[1,2048]{1,0:T(1,128)}, u32[]{:S(2)}) copy-start(f32[1,2048]{1,0:T(1,128)} %param.9) | copy-start | bytes 24580
Sparse Core Ops, SparseCore 0:
  9.6 14.8 all-gather.3
  26.0 389.7 all-gather.5
  485.6 368.8 reduce-scatter.1
